TPU v7x, 32 devices: a whole 2x2x4 slice. The times are simulated.
32 devices in a mesh: region: 4 (over z), member: 8 (over y, x, core).
Axes of the slice: x: 2, y: 2, z: 4, core: 2. Of those that a mesh axis runs over, the one named last changes fastest.
Arguments:
- ensemble: float32 [256, 1024], P('member', 'region'), may hold values from -6 to 6
- obs_value: float32 [2048], replicated, may hold values from -6 to 6
- obs_error: float32 [2048], replicated, may hold values from 0.5 to 2
- obs_region: int32 [2048], replicated, may hold values from 0 to 3
- obs_cell: int32 [2048], replicated, may hold values from 0 to 255
- order: int32 [2048], replicated, may hold values from 0 to 2047, each once
- footprint: int32 [2, 8, 2], P(None, 'region'), may hold values from 0 to 15, as said below
Outputs:
- analysis: float32 [256, 1024], P('member', 'region')
Inputs may be any that keep to these rules, and one draw needn't show every extreme that they name: `footprint`: the 2 observation tiles listed for one state tile and batch are different.
All inputs are finite; a program needn't handle non-finite values.
Results may differ from a plain program's by a relative error of at most 0.0003.
Values sent between devices are 32-bit elements; how exact they have to be, the bound alone decides.
A program may use at most 64 MiB of HBM per device.

v0:
```python
import jax
import jax.numpy as jnp
from jax import lax
from jax.sharding import PartitionSpec as P

NOBS = 1024
BATCHES = 2
STILE = 128
OTILE = 64
FOOT = 2


def per_device(ensemble, obs_value, obs_error, obs_region, obs_cell, order, footprint):
    mem_dev, cell_count = ensemble.shape
    members = mem_dev * lax.axis_size("member")
    tile_count = cell_count // STILE
    state = ensemble
    region = lax.axis_index("region")
    offsets = jnp.arange(OTILE, dtype=jnp.int32)
    for batch_no in range(BATCHES):
        chosen = order[batch_no * NOBS : (batch_no + 1) * NOBS]
        owned_here = obs_region[chosen] == region
        picked = jnp.where(owned_here[None, :], jnp.take(state, obs_cell[chosen], axis=1), 0.0)
        priors = lax.psum(picked, "region")
        obs_index = (footprint[batch_no][:, :, None] * OTILE + offsets[None, None, :]).reshape(
            tile_count, FOOT * OTILE
        )
        state_tiles = state.reshape(mem_dev, tile_count, STILE)
        s_one = jnp.sum(priors, axis=0)
        s_two = jnp.sum(priors * priors, axis=0)
        s_one, s_two = lax.psum((s_one, s_two), "member")
        obs_mean = s_one / members
        obs_pert = priors - obs_mean[None, :]
        obs_tiles = jnp.take(obs_pert, obs_index, axis=1)
        partial_value = jnp.einsum(
            "mtj,mtc->tjc", obs_tiles, state_tiles, precision=lax.Precision.HIGHEST
        )
        summed = lax.psum(partial_value, "member")
        covariance = summed / (members - 1)
        obs_var = (s_two - s_one * obs_mean) / (members - 1)
        err_var = obs_error[chosen]
        obs_gain = 1.0 / (obs_var + err_var)
        shrink = 1.0 / (1.0 + jnp.sqrt(err_var * obs_gain))
        innovation = obs_value[chosen] - obs_mean
        weight = covariance * obs_gain[obs_index][:, :, None]
        mean_step = jnp.einsum(
            "tjc,tj->tc", weight, innovation[obs_index], precision=lax.Precision.HIGHEST
        )
        scaled = obs_tiles * shrink[obs_index][None, :, :]
        pert_step = jnp.einsum("mtj,tjc->mtc", scaled, weight, precision=lax.Precision.HIGHEST)
        state = (
            state + mean_step.reshape(cell_count)[None, :] - pert_step.reshape(mem_dev, cell_count)
        )
    return state


def solution(mesh):
    in_specs = (P("member", "region"), P(), P(), P(), P(), P(), P(None, "region", None))
    out_specs = P("member", "region")
    return jax.shard_map(
        per_device, mesh=mesh, in_specs=in_specs, out_specs=out_specs, check_vma=False
    )
```

profile of v0, /device:TPU:0, one launch (start us, length us, event | category | flops | bytes accessed | tf_op | source)
XLA Modules:
  0.0 252.9 jit_solution(2424373004848491540)
XLA Ops:
  7.3 6.2 %gather_fusion.1 = s32[1024]{0:T(1024)S(1)} fusion(s32[2048]{0:T(1024)S(1)} %copy-done, s32[1024]{0:T(1024)S(1)} %get-tuple-element.20), kind=kCustom, calls=%fused_computation.5 | custom fusion | bytes 12288 | tf_op jit(solution)/shard_map/gather | solution.py:23
  13.4 6.2 %gather_fusion = s32[1024]{0:T(1024)S(1)} fusion(s32[2048]{0:T(1024)S(1)} %copy-done.1, s32[1024]{0:T(1024)S(1)} %get-tuple-element.20), kind=kCustom, calls=%fused_computation.4 | custom fusion | bytes 12288 | tf_op jit(solution)/shard_map/gather | solution.py:22
  19.8 2.8 %gather_fusion.14 = f32[1024,32]{1,0:T(8,128)S(1)} fusion(f32[32,256]{0,1:T(8,128)S(1)} %copy.26, s32[1024]{0:T(1024)S(1)} %fusion.34), kind=kCustom, calls=%fused_computation.clone | custom fusion | bytes 266240 | tf_op jit(solution)/shard_map/jit(_take)/gather | solution.py:23
  25.0 6.1 %gather_fusion.8 = s32[1024]{0:T(1024)S(1)} fusion(s32[2048]{0:T(1024)S(1)} %copy-done, s32[1024]{0:T(1024)S(1)} %get-tuple-element.19), kind=kCustom, calls=%fused_computation.12 | custom fusion | bytes 12288 | tf_op jit(solution)/shard_map/gather | solution.py:23
  31.1 6.2 %gather_fusion.7 = s32[1024]{0:T(1024)S(1)} fusion(s32[2048]{0:T(1024)S(1)} %copy-done.1, s32[1024]{0:T(1024)S(1)} %get-tuple-element.19), kind=kCustom, calls=%fused_computation.11 | custom fusion | bytes 12288 | tf_op jit(solution)/shard_map/gather | solution.py:22
  38.0 6.1 %gather_fusion.2 = f32[1024]{0:T(1024)S(1)} fusion(f32[2048]{0:T(1024)S(1)} %copy-done.2, s32[1024]{0:T(1024)S(1)} %get-tuple-element.20), kind=kCustom, calls=%fused_computation.6 | custom fusion | bytes 12288 | tf_op jit(solution)/shard_map/gather | solution.py:41
  44.2 6.2 %gather_fusion.4 = f32[1024]{0:T(1024)S(1)} fusion(f32[2048]{0:T(1024)S(1)} %copy-done.3, s32[1024]{0:T(1024)S(1)} %get-tuple-element.20), kind=kCustom, calls=%fused_computation.8 | custom fusion | bytes 12288 | tf_op jit(solution)/shard_map/gather | solution.py:44
  50.4 14.5 %all-reduce.7.cloned.1.call-done = f32[32,1024]{0,1:T(8,128)} async-done(((f32[32,1024]{0,1:T(8,128)}), f32[32,1024]{0,1:T(8,128)}) %all-reduce.7.cloned.1.call-update) | async-done | bytes 131088 | tf_op jit(solution)/shard_map/psum | solution.py:24
  64.9 1.4 multiply_reduce_fusion.1
  66.3 13.2 %all-reduce.1 = (f32[1024]{0:T(1024)S(1)}, f32[1024]{0:T(1024)S(1)}) all-reduce(f32[1024]{0:T(1024)S(1)} %get-tuple-element.10, f32[1024]{0:T(1024)S(1)} %get-tuple-element.9), channel_id=1, replica_groups=mesh['region'=4,'member'=8] {'member'}, use_global_device_ids=true, to_apply=%region_2.4 | all-reduce | flops 2048 | bytes 16384 | tf_op jit(solution)/shard_map/psum | solution.py:31
  81.7 1.4 gather_fusion.3
  83.1 1.4 gather_fusion.5
  84.4 1.4 gather_fusion.6
  85.8 46.9 %all-reduce.9.cloned.1.call-done = f32[2,128,128]{2,1,0:T(8,128)} async-done(((f32[2,128,128]{2,1,0:T(8,128)}), f32[2,128,128]{2,1,0:T(8,128)}) %all-reduce.9.cloned.1.call-update) | async-done | bytes 131088 | tf_op jit(solution)/shard_map/psum | solution.py:38
  134.4 2.8 %gather_fusion.16 = f32[1024,32]{1,0:T(8,128)S(1)} fusion(f32[32,256]{0,1:T(8,128)S(1)} %copy.30, s32[1024]{0:T(1024)S(1)} %fusion.35), kind=kCustom, calls=%fused_computation.2.clone | custom fusion | bytes 266240 | tf_op jit(solution)/shard_map/jit(_take)/gather | solution.py:23
  138.5 6.2 %gather_fusion.9 = f32[1024]{0:T(1024)S(1)} fusion(f32[2048]{0:T(1024)S(1)} %copy-done.2, s32[1024]{0:T(1024)S(1)} %get-tuple-element.19), kind=kCustom, calls=%fused_computation.13 | custom fusion | bytes 12288 | tf_op jit(solution)/shard_map/gather | solution.py:41
  144.6 6.2 %gather_fusion.11 = f32[1024]{0:T(1024)S(1)} fusion(f32[2048]{0:T(1024)S(1)} %copy-done.3, s32[1024]{0:T(1024)S(1)} %get-tuple-element.19), kind=kCustom, calls=%fused_computation.15 | custom fusion | bytes 12288 | tf_op jit(solution)/shard_map/gather | solution.py:44
  150.8 25.4 %all-reduce.11.cloned.1.call-done = f32[32,1024]{0,1:T(8,128)} async-done(((f32[32,1024]{0,1:T(8,128)}), f32[32,1024]{0,1:T(8,128)}) %all-reduce.11.cloned.1.call-update) | async-done | bytes 131088 | tf_op jit(solution)/shard_map/psum | solution.py:24
  176.2 1.4 multiply_reduce_fusion
  177.7 13.2 %all-reduce = (f32[1024]{0:T(1024)S(1)}, f32[1024]{0:T(1024)S(1)}) all-reduce(f32[1024]{0:T(1024)S(1)} %get-tuple-element.8, f32[1024]{0:T(1024)S(1)} %get-tuple-element.6), channel_id=1, replica_groups=mesh['region'=4,'member'=8] {'member'}, use_global_device_ids=true, to_apply=%region_8.11 | all-reduce | flops 2048 | bytes 16384 | tf_op jit(solution)/shard_map/psum | solution.py:31
  193.0 1.4 gather_fusion.10
  194.4 1.4 gather_fusion.12
  195.8 1.4 gather_fusion.13
  197.1 47.0 %all-reduce.13.cloned.1.call-done = f32[2,128,128]{2,1,0:T(8,128)} async-done(((f32[2,128,128]{2,1,0:T(8,128)}), f32[2,128,128]{2,1,0:T(8,128)}) %all-reduce.13.cloned.1.call-update) | async-done | bytes 131088 | tf_op jit(solution)/shard_map/psum | solution.py:38
  (70 shorter events, 13.3 us)
Async XLA Ops:
  6.5 0.7 copy-start
  6.5 58.3 %all-reduce.7.cloned.1.call-start = ((), (), s32[]{:S(2)}) async-start(), calls=%async_computation | async-start | bytes 1048576 | tf_op jit(solution)/shard_map/psum | solution.py:24
  7.3 6.2 %copy-start.1 = (s32[2048]{0:T(1024)S(1)}, s32[2048]{0:T(1024)}, u32[]{:S(2)}) copy-start(s32[2048]{0:T(1024)} %param.14) | copy-start | bytes 24580
  13.4 6.2 %copy-start.8 = (f32[32,256]{1,0:T(8,128)S(1)}, f32[32,256]{1,0:T(8,128)}, u32[]{:S(2)}) copy-start(f32[32,256]{1,0:T(8,128)} %param.11) | copy-start | bytes 98308
  23.7 0.7 copy-start.9
  23.7 109.0 %all-reduce.9.cloned.1.call-start = ((), (), s32[]{:S(2)}) async-start(), calls=%async_computation.1 | async-start | bytes 262144 | tf_op jit(solution)/shard_map/psum | solution.py:38
  37.3 0.7 copy-start.2
  38.0 6.2 %copy-start.3 = (f32[2048]{0:T(1024)S(1)}, f32[2048]{0:T(1024)}, u32[]{:S(2)}) copy-start(f32[2048]{0:T(1024)} %param.12) | copy-start | bytes 24580
  64.9 14.7 %copy-start.4 = (f32[32,1024]{0,1:T(8,128)S(1)}, f32[32,1024]{0,1:T(8,128)}, u32[]{:S(2)}) copy-start(f32[32,1024]{0,1:T(8,128)} %all-reduce.7.cloned.1.call-done) | copy-start | bytes 393220
  81.6 94.6 %all-reduce.11.cloned.1.call-start = ((), (), s32[]{:S(2)}) async-start(), calls=%async_computation.2 | async-start | bytes 1048576 | tf_op jit(solution)/shard_map/psum | solution.py:24
  132.7 1.3 copy-start.6
  138.4 105.7 %all-reduce.13.cloned.1.call-start = ((), (), s32[]{:S(2)}) async-start(), calls=%async_computation.3 | async-start | bytes 262144 | tf_op jit(solution)/shard_map/psum | solution.py:38
  176.2 14.7 %copy-start.5 = (f32[32,1024]{0,1:T(8,128)S(1)}, f32[32,1024]{0,1:T(8,128)}, u32[]{:S(2)}) copy-start(f32[32,1024]{0,1:T(8,128)} %all-reduce.11.cloned.1.call-done) | copy-start | bytes 393220
  244.1 1.3 copy-start.7
Sparse Core Ops, SparseCore 0:
  23.9 40.9 all-reduce.6
  81.7 50.9 all-reduce.8
  138.6 37.6 all-reduce.10
  193.1 50.9 all-reduce.12
where the time goes:
time: 253 us
  waiting for transfers between devices  134 us (53%)
  local copies, waits for them, and re-layouts  66.7 us (26%)
  blocking collectives  26.3 us (10%)
  between operations  13.5 us (5%)
  other arithmetic  7.04 us (3%)
  matrix products  5.26 us (2%)
    psum x2, waiting for transfers between devices, per_device(): summed = lax.psum(partial_value, 'member')  93.9 us
    psum x2, waiting for transfers between devices, per_device(): priors = lax.psum(picked, 'region')  39.9 us
    psum x2, blocking collectives, per_device(): s_one, s_two = lax.psum((s_one, s_two), 'member')  26.3 us
    gather x2, local copies, waits for them, and re-layouts, per_device(): owned_here = obs_region[chosen] == region  12.3 us
    gather x2, local copies, waits for them, and re-layouts, per_device(): innovation = obs_value[chosen] - obs_mean  12.3 us
    gather x2, local copies, waits for them, and re-layouts, per_device(): obs_cell[chosen]  12.3 us
    gather x2, local copies, waits for them, and re-layouts, per_device(): err_var = obs_error[chosen]  12.3 us
    gather x2, local copies, waits for them, and re-layouts, per_device(): jnp.take(state, obs_cell[chosen], axis=1)  5.64 us
  transfers between devices with their start and end apart: 4, of which 4 were waited for; matrix products, arithmetic and copies ran while one was open for 18% of the time, Pallas kernels for 0%

commit v1 on v0

--- a/solution.py
+++ b/solution.py
@@ -8,6 +8,10 @@
 STILE = 128
 OTILE = 64
 FOOT = 2
+
+
+def show_lane_in(own_rows):
+    return lax.all_gather(own_rows, axis_name="member").sum(axis=0)
 
 
 def per_device(ensemble, obs_value, obs_error, obs_region, obs_cell, order, footprint):
@@ -35,7 +39,7 @@
         partial_value = jnp.einsum(
             "mtj,mtc->tjc", obs_tiles, state_tiles, precision=lax.Precision.HIGHEST
         )
-        summed = lax.psum(partial_value, "member")
+        summed = show_lane_in(partial_value)
         covariance = summed / (members - 1)
         obs_var = (s_two - s_one * obs_mean) / (members - 1)
         err_var = obs_error[chosen]

time: 253 us -> 196 us (0.77)
  waiting for transfers between devices: 134 us -> 75.9 us
  other arithmetic: 7.04 us -> 9.64 us
    psum x2 -> x0, waiting for transfers between devices: 93.9 us -> none  [per_device(): summed = lax.psum(partial_value, 'member')]
    all_gather x0 -> x2, waiting for transfers between devices: none -> 22.5 us  [show_lane_in(): return lax.all_gather(own_rows, axis_name='member').sum(axis=0)]
    psum x2, waiting for transfers between devices: 39.9 us -> 53.3 us  [per_device(): priors = lax.psum(picked, 'region')]
    reduce_sum x0 -> x2, other arithmetic: none -> 2.59 us  [show_lane_in(): return lax.all_gather(own_rows, axis_name='member').sum(axis=0)]
  transfers between devices with their start and end apart: 4 -> 4, of which waited for: 4 -> 4; matrix products, arithmetic and copies ran while one was open for 18% -> 23% of each run, Pallas kernels for 0% -> 0%
where the time goes in v1:
time: 196 us
  waiting for transfers between devices  75.9 us (39%)
  local copies, waits for them, and re-layouts  67.1 us (34%)
  blocking collectives  26.3 us (13%)
  between operations  13.5 us (7%)
  other arithmetic  9.64 us (5%)
  matrix products  3.34 us (2%)
    psum x2, waiting for transfers between devices, per_device(): priors = lax.psum(picked, 'region')  53.3 us
    psum x2, blocking collectives, per_device(): s_one, s_two = lax.psum((s_one, s_two), 'member')  26.3 us
    all_gather x2, waiting for transfers between devices, show_lane_in(): return lax.all_gather(own_rows, axis_name='member').sum(axis=0)  22.5 us
    gather x2, local copies, waits for them, and re-layouts, per_device(): err_var = obs_error[chosen]  12.3 us
    gather x2, local copies, waits for them, and re-layouts, per_device(): owned_here = obs_region[chosen] == region  12.3 us
    gather x2, local copies, waits for them, and re-layouts, per_device(): innovation = obs_value[chosen] - obs_mean  12.3 us
    gather x2, local copies, waits for them, and re-layouts, per_device(): obs_cell[chosen]  12.3 us
    gather x2, local copies, waits for them, and re-layouts, per_device(): jnp.take(state, obs_cell[chosen], axis=1)  5.64 us
  transfers between devices with their start and end apart: 4, of which 4 were waited for; matrix products, arithmetic and copies ran while one was open for 23% of the time, Pallas kernels for 0%

profile of v1, /device:TPU:0, one launch (start us, length us, event | category | flops | bytes accessed | tf_op | source)
XLA Modules:
  0.0 195.9 jit_solution(5111954408993964318)
XLA Ops:
  7.3 6.1 %gather_fusion.1 = s32[1024]{0:T(1024)S(1)} fusion(s32[2048]{0:T(1024)S(1)} %copy-done, s32[1024]{0:T(1024)S(1)} %get-tuple-element.20), kind=kCustom, calls=%fused_computation.5 | custom fusion | bytes 12288 | tf_op jit(solution)/shard_map/gather | solution.py:27
  14.1 6.1 %gather_fusion = s32[1024]{0:T(1024)S(1)} fusion(s32[2048]{0:T(1024)S(1)} %copy-done.1, s32[1024]{0:T(1024)S(1)} %get-tuple-element.20), kind=kCustom, calls=%fused_computation.4 | custom fusion | bytes 12288 | tf_op jit(solution)/shard_map/gather | solution.py:26
  20.4 2.8 %gather_fusion.14 = f32[1024,32]{1,0:T(8,128)S(1)} fusion(f32[32,256]{0,1:T(8,128)S(1)} %copy.37, s32[1024]{0:T(1024)S(1)} %fusion.34), kind=kCustom, calls=%fused_computation.clone | custom fusion | bytes 266240 | tf_op jit(solution)/shard_map/jit(_take)/gather | solution.py:27
  25.9 6.1 %gather_fusion.4 = f32[1024]{0:T(1024)S(1)} fusion(f32[2048]{0:T(1024)S(1)} %copy-done.2, s32[1024]{0:T(1024)S(1)} %get-tuple-element.20), kind=kCustom, calls=%fused_computation.8 | custom fusion | bytes 12288 | tf_op jit(solution)/shard_map/gather | solution.py:48
  32.1 6.2 %gather_fusion.2 = f32[1024]{0:T(1024)S(1)} fusion(f32[2048]{0:T(1024)S(1)} %copy-done.3, s32[1024]{0:T(1024)S(1)} %get-tuple-element.20), kind=kCustom, calls=%fused_computation.6 | custom fusion | bytes 12288 | tf_op jit(solution)/shard_map/gather | solution.py:45
  38.3 27.2 %all-reduce.5.cloned.1.call-done = f32[32,1024]{0,1:T(8,128)} async-done(((f32[32,1024]{0,1:T(8,128)}), f32[32,1024]{0,1:T(8,128)}) %all-reduce.5.cloned.1.call-update) | async-done | bytes 131088 | tf_op jit(solution)/shard_map/psum | solution.py:28
  65.5 1.4 multiply_reduce_fusion.1
  67.0 13.2 %all-reduce.1 = (f32[1024]{0:T(1024)S(1)}, f32[1024]{0:T(1024)S(1)}) all-reduce(f32[1024]{0:T(1024)S(1)} %get-tuple-element.10, f32[1024]{0:T(1024)S(1)} %get-tuple-element.9), channel_id=1, replica_groups=mesh['region'=4,'member'=8] {'member'}, use_global_device_ids=true, to_apply=%region_2.4 | all-reduce | flops 2048 | bytes 16384 | tf_op jit(solution)/shard_map/psum | solution.py:35
  82.5 6.1 %gather_fusion.8 = s32[1024]{0:T(1024)S(1)} fusion(s32[2048]{0:T(1024)S(1)} %copy-done, s32[1024]{0:T(1024)S(1)} %get-tuple-element.19), kind=kCustom, calls=%fused_computation.12 | custom fusion | bytes 12288 | tf_op jit(solution)/shard_map/gather | solution.py:27
  88.6 6.2 %gather_fusion.7 = s32[1024]{0:T(1024)S(1)} fusion(s32[2048]{0:T(1024)S(1)} %copy-done.1, s32[1024]{0:T(1024)S(1)} %get-tuple-element.19), kind=kCustom, calls=%fused_computation.11 | custom fusion | bytes 12288 | tf_op jit(solution)/shard_map/gather | solution.py:26
  94.8 1.4 gather_fusion.6
  96.2 1.4 gather_fusion.3
  97.6 1.4 gather_fusion.5
  99.0 5.0 %all-gather.5.cloned.1.call-done = f32[16,128,128]{2,1,0:T(8,128)} async-done(((f32[2,128,128]{2,1,0:T(8,128)}), f32[16,128,128]{2,1,0:T(8,128)}) %all-gather.5.cloned.1.call-update) | async-done | bytes 1048592 | tf_op jit(solution)/shard_map/all_gather | solution.py:14
  106.0 2.8 %gather_fusion.16 = f32[1024,32]{1,0:T(8,128)S(1)} fusion(f32[32,256]{0,1:T(8,128)S(1)} %copy.41, s32[1024]{0:T(1024)S(1)} %fusion.35), kind=kCustom, calls=%fused_computation.2.clone | custom fusion | bytes 266240 | tf_op jit(solution)/shard_map/jit(_take)/gather | solution.py:27
  110.0 6.2 %gather_fusion.11 = f32[1024]{0:T(1024)S(1)} fusion(f32[2048]{0:T(1024)S(1)} %copy-done.2, s32[1024]{0:T(1024)S(1)} %get-tuple-element.19), kind=kCustom, calls=%fused_computation.15 | custom fusion | bytes 12288 | tf_op jit(solution)/shard_map/gather | solution.py:48
  116.2 6.2 %gather_fusion.9 = f32[1024]{0:T(1024)S(1)} fusion(f32[2048]{0:T(1024)S(1)} %copy-done.3, s32[1024]{0:T(1024)S(1)} %get-tuple-element.19), kind=kCustom, calls=%fused_computation.13 | custom fusion | bytes 12288 | tf_op jit(solution)/shard_map/gather | solution.py:45
  122.3 26.0 %all-reduce.7.cloned.1.call-done = f32[32,1024]{0,1:T(8,128)} async-done(((f32[32,1024]{0,1:T(8,128)}), f32[32,1024]{0,1:T(8,128)}) %all-reduce.7.cloned.1.call-update) | async-done | bytes 131088 | tf_op jit(solution)/shard_map/psum | solution.py:28
  148.4 1.4 multiply_reduce_fusion
  149.8 13.2 %all-reduce = (f32[1024]{0:T(1024)S(1)}, f32[1024]{0:T(1024)S(1)}) all-reduce(f32[1024]{0:T(1024)S(1)} %get-tuple-element.8, f32[1024]{0:T(1024)S(1)} %get-tuple-element.6), channel_id=1, replica_groups=mesh['region'=4,'member'=8] {'member'}, use_global_device_ids=true, to_apply=%region_8.11 | all-reduce | flops 2048 | bytes 16384 | tf_op jit(solution)/shard_map/psum | solution.py:35
  165.1 1.4 gather_fusion.13
  166.5 1.4 gather_fusion.10
  167.9 1.4 gather_fusion.12
  169.3 17.6 %all-gather.7.cloned.1.call-done = f32[16,128,128]{2,1,0:T(8,128)} async-done(((f32[2,128,128]{2,1,0:T(8,128)}), f32[16,128,128]{2,1,0:T(8,128)}) %all-gather.7.cloned.1.call-update) | async-done | bytes 1048592 | tf_op jit(solution)/shard_map/all_gather | solution.py:14
  (68 shorter events, 14.4 us)
Async XLA Ops:
  6.5 0.7 copy-start
  6.5 59.0 %all-reduce.5.cloned.1.call-start = ((), (), s32[]{:S(2)}) async-start(), calls=%async_computation | async-start | bytes 1048576 | tf_op jit(solution)/shard_map/psum | solution.py:28
  13.4 0.7 copy-start.1
  14.1 6.2 %copy-start.6 = (f32[32,256]{1,0:T(8,128)S(1)}, f32[32,256]{1,0:T(8,128)}, u32[]{:S(2)}) copy-start(f32[32,256]{1,0:T(8,128)} %param.11) | copy-start | bytes 98308
  24.4 0.7 copy-start.7
  24.4 79.5 %all-gather.5.cloned.1.call-start = ((), (), s32[]{:S(2)}) async-start(), calls=%async_computation.2 | async-start | bytes 1179648 | tf_op jit(solution)/shard_map/all_gather | solution.py:14
  25.2 0.7 copy-start.2
  25.9 6.2 %copy-start.3 = (f32[2048]{0:T(1024)S(1)}, f32[2048]{0:T(1024)}, u32[]{:S(2)}) copy-start(f32[2048]{0:T(1024)} %param.13) | copy-start | bytes 24580
  65.5 14.7 %copy-start.4 = (f32[32,1024]{0,1:T(8,128)S(1)}, f32[32,1024]{0,1:T(8,128)}, u32[]{:S(2)}) copy-start(f32[32,1024]{0,1:T(8,128)} %all-reduce.5.cloned.1.call-done) | copy-start | bytes 393220
  82.3 66.1 %all-reduce.7.cloned.1.call-start = ((), (), s32[]{:S(2)}) async-start(), calls=%async_computation.1 | async-start | bytes 1048576 | tf_op jit(solution)/shard_map/psum | solution.py:28
  110.0 76.9 %all-gather.7.cloned.1.call-start = ((), (), s32[]{:S(2)}) async-start(), calls=%async_computation.3 | async-start | bytes 1179648 | tf_op jit(solution)/shard_map/all_gather | solution.py:14
  148.4 14.7 %copy-start.5 = (f32[32,1024]{0,1:T(8,128)S(1)}, f32[32,1024]{0,1:T(8,128)}, u32[]{:S(2)}) copy-start(f32[32,1024]{0,1:T(8,128)} %all-reduce.7.cloned.1.call-done) | copy-start | bytes 393220
Sparse Core Ops, SparseCore 0:
  24.5 40.9 all-reduce.4
  82.4 21.5 all-gather.4
  110.1 38.2 all-reduce.6
  165.3 21.5 all-gather.6
